TPU v7x, 32 devices: a whole 2x2x4 slice. The times are simulated.
32 devices in a mesh: group: 4 (over y, core), shard: 8 (over z, x).
Axes of the slice: x: 2, y: 2, z: 4, core: 2. Of those that a mesh axis runs over, the one named last changes fastest.
Arguments:
- queries: bfloat16 [512, 32, 128], P(('group', 'shard')), may hold values from -12 to 12
- passages: bfloat16 [2048, 64, 128], P(('group', 'shard')), may hold values from -4 to 4
- candidates: int32 [512, 160], P(('group', 'shard')), may hold values from 0 to 2047, as said below
- passage_slot: int32 [2048], replicated, may hold values from 0 to 2047, as said below
Outputs:
- scores: float32 [512, 160], P(('group', 'shard'))
Inputs may be any that keep to these rules, and one draw needn't show every extreme that they name: `passage_slot`: every storage row is named by exactly one passage id. `candidates`: candidates k * 20 to (k + 1) * 20 - 1 of a query, for k < 8, all lie in the storage rows of one device, rows d * 64 to (d + 1) * 64 - 1 of device d counted group-major. Over the 16 queries of one device, at most 12 such groups name any one device, and some devices are named exactly 12 times by the queries of every device.
All inputs are finite; a program needn't handle non-finite values.
Results may differ from a plain program's by a relative error of at most 0.0003.
Values may be sent and summed in bfloat16 or wider, within the bound.
No kernel may reach another device: no remote copies, remote signals or barrier semaphores. Data moves between devices by JAX's collectives and lax.ppermute only.
A program may use at most 64 MiB of HBM per device.

v0:
```python
import jax
import jax.numpy as jnp
from jax import lax
from jax.sharding import PartitionSpec as P

PER_VISIT = 20


def score_visits(query_rows, local_rows, passages):
    item_count, peer_width, qtok_count, dim_count = query_rows.shape
    slot_count, ptok_count = (passages.shape[0], passages.shape[1])
    visit_total = item_count * peer_width
    block_size = 16
    store_flat = passages.reshape(slot_count * ptok_count, dim_count)
    query_blocks = query_rows.reshape(visit_total // block_size, block_size, qtok_count, dim_count)
    row_blocks = local_rows.reshape(visit_total // block_size, block_size, local_rows.shape[2])
    slot_ids = jnp.arange(slot_count, dtype=jnp.int32)

    def one_block(pieces):
        query_block, row_block = pieces
        similarity = jnp.einsum(
            "vqd,sd->vqs", query_block, store_flat, preferred_element_type=jnp.float32
        )
        best_match = jnp.max(
            similarity.reshape(block_size, qtok_count, slot_count, ptok_count), axis=3
        )
        passage_score = jnp.sum(best_match, axis=1) / qtok_count
        picker = (row_block[:, :, None] == slot_ids[None, None, :]).astype(jnp.float32)
        return jnp.sum(picker * passage_score[:, None, :], axis=2)

    visit_scores = lax.map(one_block, (query_blocks, row_blocks))
    visit_scores = visit_scores.reshape(item_count, peer_width, local_rows.shape[2])
    return lax.all_to_all(visit_scores, ("group", "shard"), split_axis=1, concat_axis=1, tiled=True)


def local(queries, passages, candidates, passage_slot):
    peer_count = lax.axis_size(("group", "shard"))
    query_count, cand_count = candidates.shape
    slot_count = passages.shape[0]
    spread_count = cand_count // PER_VISIT
    capacity = 3 * query_count * spread_count // peer_count
    visit_count = query_count * spread_count
    storage = passage_slot[candidates].reshape(visit_count, PER_VISIT)
    target = storage[:, 0] // slot_count
    local_rows = storage % slot_count
    matches = (target[:, None] == jnp.arange(peer_count, dtype=jnp.int32)[None, :]).astype(
        jnp.int32
    )
    before = jnp.cumsum(matches, axis=0) - matches
    rank_in = jnp.sum(before * matches, axis=1)
    position = rank_in * peer_count + target
    holder = (
        jnp.zeros((capacity * peer_count,), jnp.int32)
        .at[position]
        .set(jnp.arange(visit_count, dtype=jnp.int32))
    )
    send_local = local_rows[holder].reshape(capacity, peer_count, PER_VISIT)
    query_local = holder // spread_count
    everyone = lax.all_gather(queries, ("group", "shard"), axis=0, tiled=True)
    query_global = (lax.axis_index(("group", "shard")) * query_count + query_local).reshape(
        capacity, peer_count
    )
    wanted = lax.all_to_all(
        query_global, ("group", "shard"), split_axis=1, concat_axis=1, tiled=True
    )
    local_block = lax.all_to_all(
        send_local, ("group", "shard"), split_axis=1, concat_axis=1, tiled=True
    )
    returned = score_visits(everyone[wanted], local_block, passages)
    flat_scores = returned.reshape(capacity * peer_count, PER_VISIT)[position]
    return flat_scores.reshape(query_count, cand_count)


def solution(mesh):
    return jax.shard_map(
        local,
        mesh=mesh,
        in_specs=(
            P(("group", "shard"), None, None),
            P(("group", "shard"), None, None),
            P(("group", "shard"), None),
            P(),
        ),
        out_specs=P(("group", "shard"), None),
        check_vma=False,
    )
```

profile of v0, /device:TPU:0, one launch (start us, length us, event | category | flops | bytes accessed | tf_op | source)
XLA Modules:
  0.0 248.6 jit_solution(6655536599872342939)
XLA Ops:
  6.5 0.7 all-gather.2.cloned.1.call-update
  7.3 0.7 compare_select_fusion.2
  8.1 13.6 %gather_fusion = s32[2560]{0:T(1024)S(1)} fusion(s32[2048]{0:T(1024)S(1)} %copy-done, s32[3072]{0:T(1024)S(1)} %pad_clamp_fusion), kind=kCustom, calls=%fused_computation | custom fusion | bytes 30720 | tf_op jit(solution)/shard_map/gather | solution.py:43
  22.7 1.0 scatter_custom_fusion
  23.7 0.7 copy.19
  24.4 7.3 %all-to-all-start.1 = ((s32[12,32,1]{0,2,1:T(1,128)}), s32[12,32,1]{0,2,1:T(1,128)S(1)}, u32[]{:S(2)}, u32[]{:S(2)}) async-start(s32[12,32,1]{0,2,1:T(1,128)} %copy.19), calls=%async_computation.1 | async-start | bytes 32768 | tf_op jit(solution)/shard_map/all_to_all | solution.py:63
  31.8 1.1 gather_fusion.1
  33.1 0.8 reshape.105
  33.9 5.0 %all-to-all-done.1 = s32[12,32,1]{0,2,1:T(1,128)S(1)} async-done(((s32[12,32,1]{0,2,1:T(1,128)}), s32[12,32,1]{0,2,1:T(1,128)S(1)}, u32[]{:S(2)}, u32[]{:S(2)}) %all-to-all-start.1) | async-done | bytes 1568 | tf_op jit(solution)/shard_map/all_to_all | solution.py:63
  38.8 2.5 %all-to-all-start = ((s32[32,1,240]{2,1,0:T(1,128)}), s32[32,1,240]{2,1,0:T(1,128)S(1)}, u32[]{:S(2)}, u32[]{:S(2)}) async-start(s32[32,1,240]{2,1,0:T(1,128)} %reshape.105), calls=%async_computation | async-start | bytes 65536 | tf_op jit(solution)/shard_map/all_to_all | solution.py:66
  41.6 7.0 %all-to-all-done = s32[32,1,240]{2,1,0:T(1,128)S(1)} async-done(((s32[32,1,240]{2,1,0:T(1,128)}), s32[32,1,240]{2,1,0:T(1,128)S(1)}, u32[]{:S(2)}, u32[]{:S(2)}) %all-to-all-start) | async-done | bytes 30752 | tf_op jit(solution)/shard_map/all_to_all | solution.py:66
  48.6 0.5 broadcast.107
  49.1 0.7 reduce.4
  50.1 24.7 %all-gather.2.cloned.1.call-done = bf16[512,32,128]{2,1,0:T(8,128)(2,1)} async-done(((bf16[16,32,128]{2,1,0:T(8,128)(2,1)}), bf16[512,32,128]{2,1,0:T(8,128)(2,1)}) %all-gather.2.cloned.1.call-update) | async-done | bytes 4194320 | tf_op jit(solution)/shard_map/all_gather | solution.py:59
  74.8 4.9 %gather_fusion.2 = bf16[384,32,128]{2,1,0:T(8,128)(2,1)} fusion(bf16[512,32,128]{2,1,0:T(8,128)(2,1)} %all-gather.2.cloned.1.call-done, s32[1024]{0:T(1024)S(1)} %pad_clamp_fusion.2), kind=kCustom, calls=%fused_computation.2 | custom fusion | bytes 6292992 | tf_op jit(solution)/shard_map/gather | solution.py:69
  79.7 147.7 %while.11 = (s32[]{:T(128)}, f32[24,16,20]{2,1,0:T(8,128)S(1)}, s32[24,16,20]{2,1,0:T(8,128)S(1)}, bf16[24,16,32,128]{3,2,1,0:T(8,128)(2,1)}, bf16[4096,128]{1,0:T(8,128)(2,1)S(1)}, /*index=5*/s32[]{:T(128)}, f32[]{:T(128)}) while((s32[]{:T(128)}, f32[24,16,20]{2,1,0:T(8,128)S(1)}, s32[24,16,20]{2,1,0:T(8,128)S(1)}, ...), condition=%wide.region_7.8_spmd.clone, body=%wide.region_3.7_spmd.clone.sunk | while | flops 539029184 | bytes 1484901 | solution.py:31
  79.8 5.5 %convolution_reduce_fusion.2 = f32[16,32,64]{1,2,0:T(8,128)S(1)} fusion(bf16[64,64,128,1]{2,1,0,3:T(8,128)(2,1)S(1)} %bitcast.53, bf16[24,16,32,128]{3,2,1,0:T(8,128)(2,1)} %get-tuple-element.110, s32[]{:T(128)S(6)} %copy.35), kind=kOutput, calls=%fused_computation.6.clone.1 | convolution fusion | flops 538935296 | bytes 1310724 | tf_op jit(solution)/shard_map/while/body/eval_jaxpr/vqd,sd->vqs/dot_general | solution.py:21
  85.4 0.2 reduce_sum.35
  86.0 5.5 %convolution_reduce_fusion.2 = f32[16,32,64]{1,2,0:T(8,128)S(1)} fusion(bf16[64,64,128,1]{2,1,0,3:T(8,128)(2,1)S(1)} %bitcast.53, bf16[24,16,32,128]{3,2,1,0:T(8,128)(2,1)} %get-tuple-element.110, s32[]{:T(128)S(6)} %copy.35), kind=kOutput, calls=%fused_computation.6.clone.1 | convolution fusion | flops 538935296 | bytes 1310724 | tf_op jit(solution)/shard_map/while/body/eval_jaxpr/vqd,sd->vqs/dot_general | solution.py:21
  91.5 0.2 reduce_sum.35
  92.1 5.5 %convolution_reduce_fusion.2 = f32[16,32,64]{1,2,0:T(8,128)S(1)} fusion(bf16[64,64,128,1]{2,1,0,3:T(8,128)(2,1)S(1)} %bitcast.53, bf16[24,16,32,128]{3,2,1,0:T(8,128)(2,1)} %get-tuple-element.110, s32[]{:T(128)S(6)} %copy.35), kind=kOutput, calls=%fused_computation.6.clone.1 | convolution fusion | flops 538935296 | bytes 1310724 | tf_op jit(solution)/shard_map/while/body/eval_jaxpr/vqd,sd->vqs/dot_general | solution.py:21
  97.7 0.2 reduce_sum.35
  98.3 5.5 %convolution_reduce_fusion.2 = f32[16,32,64]{1,2,0:T(8,128)S(1)} fusion(bf16[64,64,128,1]{2,1,0,3:T(8,128)(2,1)S(1)} %bitcast.53, bf16[24,16,32,128]{3,2,1,0:T(8,128)(2,1)} %get-tuple-element.110, s32[]{:T(128)S(6)} %copy.35), kind=kOutput, calls=%fused_computation.6.clone.1 | convolution fusion | flops 538935296 | bytes 1310724 | tf_op jit(solution)/shard_map/while/body/eval_jaxpr/vqd,sd->vqs/dot_general | solution.py:21
  103.9 0.2 reduce_sum.35
  104.5 5.5 %convolution_reduce_fusion.2 = f32[16,32,64]{1,2,0:T(8,128)S(1)} fusion(bf16[64,64,128,1]{2,1,0,3:T(8,128)(2,1)S(1)} %bitcast.53, bf16[24,16,32,128]{3,2,1,0:T(8,128)(2,1)} %get-tuple-element.110, s32[]{:T(128)S(6)} %copy.35), kind=kOutput, calls=%fused_computation.6.clone.1 | convolution fusion | flops 538935296 | bytes 1310724 | tf_op jit(solution)/shard_map/while/body/eval_jaxpr/vqd,sd->vqs/dot_general | solution.py:21
  110.0 0.2 reduce_sum.35
  110.6 5.5 %convolution_reduce_fusion.2 = f32[16,32,64]{1,2,0:T(8,128)S(1)} fusion(bf16[64,64,128,1]{2,1,0,3:T(8,128)(2,1)S(1)} %bitcast.53, bf16[24,16,32,128]{3,2,1,0:T(8,128)(2,1)} %get-tuple-element.110, s32[]{:T(128)S(6)} %copy.35), kind=kOutput, calls=%fused_computation.6.clone.1 | convolution fusion | flops 538935296 | bytes 1310724 | tf_op jit(solution)/shard_map/while/body/eval_jaxpr/vqd,sd->vqs/dot_general | solution.py:21
  116.2 0.2 reduce_sum.35
  116.8 5.5 %convolution_reduce_fusion.2 = f32[16,32,64]{1,2,0:T(8,128)S(1)} fusion(bf16[64,64,128,1]{2,1,0,3:T(8,128)(2,1)S(1)} %bitcast.53, bf16[24,16,32,128]{3,2,1,0:T(8,128)(2,1)} %get-tuple-element.110, s32[]{:T(128)S(6)} %copy.35), kind=kOutput, calls=%fused_computation.6.clone.1 | convolution fusion | flops 538935296 | bytes 1310724 | tf_op jit(solution)/shard_map/while/body/eval_jaxpr/vqd,sd->vqs/dot_general | solution.py:21
  122.3 0.2 reduce_sum.35
  122.9 5.5 %convolution_reduce_fusion.2 = f32[16,32,64]{1,2,0:T(8,128)S(1)} fusion(bf16[64,64,128,1]{2,1,0,3:T(8,128)(2,1)S(1)} %bitcast.53, bf16[24,16,32,128]{3,2,1,0:T(8,128)(2,1)} %get-tuple-element.110, s32[]{:T(128)S(6)} %copy.35), kind=kOutput, calls=%fused_computation.6.clone.1 | convolution fusion | flops 538935296 | bytes 1310724 | tf_op jit(solution)/shard_map/while/body/eval_jaxpr/vqd,sd->vqs/dot_general | solution.py:21
  128.5 0.2 reduce_sum.35
  129.1 5.5 %convolution_reduce_fusion.2 = f32[16,32,64]{1,2,0:T(8,128)S(1)} fusion(bf16[64,64,128,1]{2,1,0,3:T(8,128)(2,1)S(1)} %bitcast.53, bf16[24,16,32,128]{3,2,1,0:T(8,128)(2,1)} %get-tuple-element.110, s32[]{:T(128)S(6)} %copy.35), kind=kOutput, calls=%fused_computation.6.clone.1 | convolution fusion | flops 538935296 | bytes 1310724 | tf_op jit(solution)/shard_map/while/body/eval_jaxpr/vqd,sd->vqs/dot_general | solution.py:21
  135.2 5.5 %convolution_reduce_fusion.2 = f32[16,32,64]{1,2,0:T(8,128)S(1)} fusion(bf16[64,64,128,1]{2,1,0,3:T(8,128)(2,1)S(1)} %bitcast.53, bf16[24,16,32,128]{3,2,1,0:T(8,128)(2,1)} %get-tuple-element.110, s32[]{:T(128)S(6)} %copy.35), kind=kOutput, calls=%fused_computation.6.clone.1 | convolution fusion | flops 538935296 | bytes 1310724 | tf_op jit(solution)/shard_map/while/body/eval_jaxpr/vqd,sd->vqs/dot_general | solution.py:21
  140.8 0.2 reduce_sum.35
  141.4 5.5 %convolution_reduce_fusion.2 = f32[16,32,64]{1,2,0:T(8,128)S(1)} fusion(bf16[64,64,128,1]{2,1,0,3:T(8,128)(2,1)S(1)} %bitcast.53, bf16[24,16,32,128]{3,2,1,0:T(8,128)(2,1)} %get-tuple-element.110, s32[]{:T(128)S(6)} %copy.35), kind=kOutput, calls=%fused_computation.6.clone.1 | convolution fusion | flops 538935296 | bytes 1310724 | tf_op jit(solution)/shard_map/while/body/eval_jaxpr/vqd,sd->vqs/dot_general | solution.py:21
  147.5 5.5 %convolution_reduce_fusion.2 = f32[16,32,64]{1,2,0:T(8,128)S(1)} fusion(bf16[64,64,128,1]{2,1,0,3:T(8,128)(2,1)S(1)} %bitcast.53, bf16[24,16,32,128]{3,2,1,0:T(8,128)(2,1)} %get-tuple-element.110, s32[]{:T(128)S(6)} %copy.35), kind=kOutput, calls=%fused_computation.6.clone.1 | convolution fusion | flops 538935296 | bytes 1310724 | tf_op jit(solution)/shard_map/while/body/eval_jaxpr/vqd,sd->vqs/dot_general | solution.py:21
  153.1 0.2 reduce_sum.35
  153.7 5.5 %convolution_reduce_fusion.2 = f32[16,32,64]{1,2,0:T(8,128)S(1)} fusion(bf16[64,64,128,1]{2,1,0,3:T(8,128)(2,1)S(1)} %bitcast.53, bf16[24,16,32,128]{3,2,1,0:T(8,128)(2,1)} %get-tuple-element.110, s32[]{:T(128)S(6)} %copy.35), kind=kOutput, calls=%fused_computation.6.clone.1 | convolution fusion | flops 538935296 | bytes 1310724 | tf_op jit(solution)/shard_map/while/body/eval_jaxpr/vqd,sd->vqs/dot_general | solution.py:21
  159.9 5.5 %convolution_reduce_fusion.2 = f32[16,32,64]{1,2,0:T(8,128)S(1)} fusion(bf16[64,64,128,1]{2,1,0,3:T(8,128)(2,1)S(1)} %bitcast.53, bf16[24,16,32,128]{3,2,1,0:T(8,128)(2,1)} %get-tuple-element.110, s32[]{:T(128)S(6)} %copy.35), kind=kOutput, calls=%fused_computation.6.clone.1 | convolution fusion | flops 538935296 | bytes 1310724 | tf_op jit(solution)/shard_map/while/body/eval_jaxpr/vqd,sd->vqs/dot_general | solution.py:21
  165.4 0.2 reduce_sum.35
  166.0 5.5 %convolution_reduce_fusion.2 = f32[16,32,64]{1,2,0:T(8,128)S(1)} fusion(bf16[64,64,128,1]{2,1,0,3:T(8,128)(2,1)S(1)} %bitcast.53, bf16[24,16,32,128]{3,2,1,0:T(8,128)(2,1)} %get-tuple-element.110, s32[]{:T(128)S(6)} %copy.35), kind=kOutput, calls=%fused_computation.6.clone.1 | convolution fusion | flops 538935296 | bytes 1310724 | tf_op jit(solution)/shard_map/while/body/eval_jaxpr/vqd,sd->vqs/dot_general | solution.py:21
  172.2 5.5 %convolution_reduce_fusion.2 = f32[16,32,64]{1,2,0:T(8,128)S(1)} fusion(bf16[64,64,128,1]{2,1,0,3:T(8,128)(2,1)S(1)} %bitcast.53, bf16[24,16,32,128]{3,2,1,0:T(8,128)(2,1)} %get-tuple-element.110, s32[]{:T(128)S(6)} %copy.35), kind=kOutput, calls=%fused_computation.6.clone.1 | convolution fusion | flops 538935296 | bytes 1310724 | tf_op jit(solution)/shard_map/while/body/eval_jaxpr/vqd,sd->vqs/dot_general | solution.py:21
  178.3 5.5 %convolution_reduce_fusion.2 = f32[16,32,64]{1,2,0:T(8,128)S(1)} fusion(bf16[64,64,128,1]{2,1,0,3:T(8,128)(2,1)S(1)} %bitcast.53, bf16[24,16,32,128]{3,2,1,0:T(8,128)(2,1)} %get-tuple-element.110, s32[]{:T(128)S(6)} %copy.35), kind=kOutput, calls=%fused_computation.6.clone.1 | convolution fusion | flops 538935296 | bytes 1310724 | tf_op jit(solution)/shard_map/while/body/eval_jaxpr/vqd,sd->vqs/dot_general | solution.py:21
  183.9 0.2 reduce_sum.35
  184.5 5.5 %convolution_reduce_fusion.2 = f32[16,32,64]{1,2,0:T(8,128)S(1)} fusion(bf16[64,64,128,1]{2,1,0,3:T(8,128)(2,1)S(1)} %bitcast.53, bf16[24,16,32,128]{3,2,1,0:T(8,128)(2,1)} %get-tuple-element.110, s32[]{:T(128)S(6)} %copy.35), kind=kOutput, calls=%fused_computation.6.clone.1 | convolution fusion | flops 538935296 | bytes 1310724 | tf_op jit(solution)/shard_map/while/body/eval_jaxpr/vqd,sd->vqs/dot_general | solution.py:21
  190.0 0.2 reduce_sum.35
  190.6 5.5 %convolution_reduce_fusion.2 = f32[16,32,64]{1,2,0:T(8,128)S(1)} fusion(bf16[64,64,128,1]{2,1,0,3:T(8,128)(2,1)S(1)} %bitcast.53, bf16[24,16,32,128]{3,2,1,0:T(8,128)(2,1)} %get-tuple-element.110, s32[]{:T(128)S(6)} %copy.35), kind=kOutput, calls=%fused_computation.6.clone.1 | convolution fusion | flops 538935296 | bytes 1310724 | tf_op jit(solution)/shard_map/while/body/eval_jaxpr/vqd,sd->vqs/dot_general | solution.py:21
  196.2 0.2 reduce_sum.35
  196.8 5.5 %convolution_reduce_fusion.2 = f32[16,32,64]{1,2,0:T(8,128)S(1)} fusion(bf16[64,64,128,1]{2,1,0,3:T(8,128)(2,1)S(1)} %bitcast.53, bf16[24,16,32,128]{3,2,1,0:T(8,128)(2,1)} %get-tuple-element.110, s32[]{:T(128)S(6)} %copy.35), kind=kOutput, calls=%fused_computation.6.clone.1 | convolution fusion | flops 538935296 | bytes 1310724 | tf_op jit(solution)/shard_map/while/body/eval_jaxpr/vqd,sd->vqs/dot_general | solution.py:21
  202.9 5.5 %convolution_reduce_fusion.2 = f32[16,32,64]{1,2,0:T(8,128)S(1)} fusion(bf16[64,64,128,1]{2,1,0,3:T(8,128)(2,1)S(1)} %bitcast.53, bf16[24,16,32,128]{3,2,1,0:T(8,128)(2,1)} %get-tuple-element.110, s32[]{:T(128)S(6)} %copy.35), kind=kOutput, calls=%fused_computation.6.clone.1 | convolution fusion | flops 538935296 | bytes 1310724 | tf_op jit(solution)/shard_map/while/body/eval_jaxpr/vqd,sd->vqs/dot_general | solution.py:21
  208.5 0.2 reduce_sum.35
  209.1 5.5 %convolution_reduce_fusion.2 = f32[16,32,64]{1,2,0:T(8,128)S(1)} fusion(bf16[64,64,128,1]{2,1,0,3:T(8,128)(2,1)S(1)} %bitcast.53, bf16[24,16,32,128]{3,2,1,0:T(8,128)(2,1)} %get-tuple-element.110, s32[]{:T(128)S(6)} %copy.35), kind=kOutput, calls=%fused_computation.6.clone.1 | convolution fusion | flops 538935296 | bytes 1310724 | tf_op jit(solution)/shard_map/while/body/eval_jaxpr/vqd,sd->vqs/dot_general | solution.py:21
  214.7 0.2 reduce_sum.35
  215.3 5.5 %convolution_reduce_fusion.2 = f32[16,32,64]{1,2,0:T(8,128)S(1)} fusion(bf16[64,64,128,1]{2,1,0,3:T(8,128)(2,1)S(1)} %bitcast.53, bf16[24,16,32,128]{3,2,1,0:T(8,128)(2,1)} %get-tuple-element.110, s32[]{:T(128)S(6)} %copy.35), kind=kOutput, calls=%fused_computation.6.clone.1 | convolution fusion | flops 538935296 | bytes 1310724 | tf_op jit(solution)/shard_map/while/body/eval_jaxpr/vqd,sd->vqs/dot_general | solution.py:21
  220.8 0.2 reduce_sum.35
  221.4 5.5 %convolution_reduce_fusion.2 = f32[16,32,64]{1,2,0:T(8,128)S(1)} fusion(bf16[64,64,128,1]{2,1,0,3:T(8,128)(2,1)S(1)} %bitcast.53, bf16[24,16,32,128]{3,2,1,0:T(8,128)(2,1)} %get-tuple-element.110, s32[]{:T(128)S(6)} %copy.35), kind=kOutput, calls=%fused_computation.6.clone.1 | convolution fusion | flops 538935296 | bytes 1310724 | tf_op jit(solution)/shard_map/while/body/eval_jaxpr/vqd,sd->vqs/dot_general | solution.py:21
  227.6 0.8 reshape.107
  228.4 3.4 %all-to-all-start.2 = ((f32[32,1,240]{2,1,0:T(1,128)}), f32[32,1,240]{2,1,0:T(1,128)S(1)}, u32[]{:S(2)}, u32[]{:S(2)}) async-start(f32[32,1,240]{2,1,0:T(1,128)} %reshape.107), calls=%async_computation.2 | async-start | bytes 65536 | tf_op jit(solution)/shard_map/all_to_all | solution.py:33
  231.8 7.2 %all-to-all-done.2 = f32[32,1,240]{2,1,0:T(1,128)S(1)} async-done(((f32[32,1,240]{2,1,0:T(1,128)}), f32[32,1,240]{2,1,0:T(1,128)S(1)}, u32[]{:S(2)}, u32[]{:S(2)}) %all-to-all-start.2) | async-done | bytes 30752 | tf_op jit(solution)/shard_map/all_to_all | solution.py:33
  239.0 0.5 broadcast.108
  239.5 0.7 reduce.5
  240.4 0.6 gather_fusion.3
  241.1 0.7 reshape.52
  (183 shorter events, 12.5 us)
Async XLA Ops:
  6.5 1.5 copy-start
  6.5 68.3 %all-gather.2.cloned.1.call-start = ((), (), s32[]{:S(2)}) async-start(), calls=%async_computation.3 | async-start | bytes 4325376 | tf_op jit(solution)/shard_map/all_gather | solution.py:59
  24.4 14.4 %all-to-all-start.1 = ((s32[12,32,1]{0,2,1:T(1,128)}), s32[12,32,1]{0,2,1:T(1,128)S(1)}, u32[]{:S(2)}, u32[]{:S(2)}) async-start(s32[12,32,1]{0,2,1:T(1,128)} %copy.19), calls=%async_computation.1 | async-start | bytes 32768 | tf_op jit(solution)/shard_map/all_to_all | solution.py:63
  38.8 9.8 %all-to-all-start = ((s32[32,1,240]{2,1,0:T(1,128)}), s32[32,1,240]{2,1,0:T(1,128)S(1)}, u32[]{:S(2)}, u32[]{:S(2)}) async-start(s32[32,1,240]{2,1,0:T(1,128)} %reshape.105), calls=%async_computation | async-start | bytes 65536 | tf_op jit(solution)/shard_map/all_to_all | solution.py:66
  50.1 29.7 %copy-start.1 = (bf16[64,64,128]{2,1,0:T(8,128)(2,1)S(1)}, bf16[64,64,128]{2,1,0:T(8,128)(2,1)}, u32[]{:S(2)}) copy-start(bf16[64,64,128]{2,1,0:T(8,128)(2,1)} %param.7) | copy-start | bytes 3145732
  228.4 10.6 %all-to-all-start.2 = ((f32[32,1,240]{2,1,0:T(1,128)}), f32[32,1,240]{2,1,0:T(1,128)S(1)}, u32[]{:S(2)}, u32[]{:S(2)}) async-start(f32[32,1,240]{2,1,0:T(1,128)} %reshape.107), calls=%async_computation.2 | async-start | bytes 65536 | tf_op jit(solution)/shard_map/all_to_all | solution.py:33
Sparse Core Ops, SparseCore 0:
  10.3 64.4 all-gather.1
where the time goes:
time: 249 us
  matrix products  133 us (53%)
  waiting for transfers between devices  44.6 us (18%)
  local copies, waits for them, and re-layouts  30.6 us (12%)
  between operations  13.6 us (5%)
  starting transfers between devices  13.3 us (5%)
  other arithmetic  12.9 us (5%)
    dot_general x24, matrix products, one_block(): jnp.einsum('vqd,sd->vqs', query_block, store_flat, preferred_element_type...  133 us
    all_gather x1, waiting for transfers between devices, local(): everyone = lax.all_gather(queries, ('group', 'shard'), axis=0, tiled=True)  24.7 us
    gather x1, local copies, waits for them, and re-layouts, local(): storage = passage_slot[candidates].reshape(visit_count, PER_VISIT)  13.6 us
    all_to_all x1, starting transfers between devices, local(): lax.all_to_all(query_global, ('group', 'shard'), split_axis=1, concat_axi...  7.33 us
    all_to_all x1, waiting for transfers between devices, score_visits(): lax.all_to_all(visit_scores, ('group', 'shard'), split_axis=1, concat_axi...  7.18 us
    all_to_all x1, waiting for transfers between devices, local(): lax.all_to_all(send_local, ('group', 'shard'), split_axis=1, concat_axis=...  7.04 us
    reduce_sum x24, other arithmetic, one_block(): passage_score = jnp.sum(best_match, axis=1) / qtok_count  5.03 us
    all_to_all x1, waiting for transfers between devices, local(): lax.all_to_all(query_global, ('group', 'shard'), split_axis=1, concat_axi...  4.98 us
  transfers between devices with their start and end apart: 4, of which 4 were waited for; matrix products, arithmetic and copies ran while one was open for 8% of the time, Pallas kernels for 0%

commit v1 on v0

--- a/solution.py
+++ b/solution.py
@@ -56,7 +56,15 @@
     )
     send_local = local_rows[holder].reshape(capacity, peer_count, PER_VISIT)
     query_local = holder // spread_count
-    everyone = lax.all_gather(queries, ("group", "shard"), axis=0, tiled=True)
+    ways, here = (lax.axis_size(("group", "shard")), lax.axis_index(("group", "shard")))
+    grown, reach = (queries, 1)
+    while reach < ways:
+        theirs = lax.ppermute(grown, ("group", "shard"), [(d, d ^ reach) for d in range(ways)])
+        mine_first = jnp.concatenate([grown, theirs], axis=0)
+        theirs_first = jnp.concatenate([theirs, grown], axis=0)
+        grown = jnp.where(here & reach == 0, mine_first, theirs_first)
+        reach = 2 * reach
+    everyone = grown
     query_global = (lax.axis_index(("group", "shard")) * query_count + query_local).reshape(
         capacity, peer_count
     )

time: 249 us -> 278 us (1.12)
  waiting for transfers between devices: 44.6 us -> 71.5 us
  between operations: 13.6 us -> 0.25 us
  starting transfers between devices: 13.3 us -> 21.6 us
  other arithmetic: 12.9 us -> 19.5 us
    ppermute x0 -> x5, waiting for transfers between devices: none -> 33.9 us  [local(): lax.ppermute(grown, ('group', 'shard'), [(d, d ^ reach) for d in range(wa...]
    all_gather x1 -> x0, waiting for transfers between devices: 24.7 us -> none  [local(): everyone = lax.all_gather(queries, ('group', 'shard'), axis=0, tiled=True)]
    all_to_all x1, waiting for transfers between devices: 4.98 us -> 23.4 us  [local(): lax.all_to_all(query_global, ('group', 'shard'), split_axis=1, concat_axi...]
    ppermute x0 -> x5, starting transfers between devices: none -> 8.84 us  [local(): lax.ppermute(grown, ('group', 'shard'), [(d, d ^ reach) for d in range(wa...]
    select_n x0 -> x5, other arithmetic: none -> 7.34 us  [local(): grown = jnp.where(here & reach == 0, mine_first, theirs_first)]
    all_to_all x1, starting transfers between devices: 2.55 us -> 5.43 us  [local(): lax.all_to_all(send_local, ('group', 'shard'), split_axis=1, concat_axis=...]
  transfers between devices with their start and end apart: 4 -> 8, of which waited for: 4 -> 7; matrix products, arithmetic and copies ran while one was open for 8% -> 7% of each run, Pallas kernels for 0% -> 0%
where the time goes in v1:
time: 278 us
  matrix products  133 us (48%)
  waiting for transfers between devices  71.5 us (26%)
  local copies, waits for them, and re-layouts  30.8 us (11%)
  starting transfers between devices  21.6 us (8%)
  other arithmetic  19.5 us (7%)
    dot_general x24, matrix products, one_block(): jnp.einsum('vqd,sd->vqs', query_block, store_flat, preferred_element_type...  133 us
    ppermute x5, waiting for transfers between devices, local(): lax.ppermute(grown, ('group', 'shard'), [(d, d ^ reach) for d in range(wa...  33.9 us
    all_to_all x1, waiting for transfers between devices, local(): lax.all_to_all(query_global, ('group', 'shard'), split_axis=1, concat_axi...  23.4 us
    gather x1, local copies, waits for them, and re-layouts, local(): storage = passage_slot[candidates].reshape(visit_count, PER_VISIT)  13.6 us
    ppermute x5, starting transfers between devices, local(): lax.ppermute(grown, ('group', 'shard'), [(d, d ^ reach) for d in range(wa...  8.84 us
    select_n x5, other arithmetic, local(): grown = jnp.where(here & reach == 0, mine_first, theirs_first)  7.34 us
    all_to_all x1, waiting for transfers between devices, score_visits(): lax.all_to_all(visit_scores, ('group', 'shard'), split_axis=1, concat_axi...  7.18 us
    all_to_all x1, waiting for transfers between devices, local(): lax.all_to_all(send_local, ('group', 'shard'), split_axis=1, concat_axis=...  6.99 us
  transfers between devices with their start and end apart: 8, of which 7 were waited for; matrix products, arithmetic and copies ran while one was open for 7% of the time, Pallas kernels for 0%

profile of v1, /device:TPU:0, one launch (start us, length us, event | category | flops | bytes accessed | tf_op | source)
XLA Modules:
  0.0 277.5 jit_solution(18371286640700831930)
XLA Ops:
  0.0 3.0 %collective-permute-start = (bf16[16,32,128]{2,1,0:T(8,128)(2,1)}, bf16[16,32,128]{2,1,0:T(8,128)(2,1)S(1)}, u32[]{:S(2)}, u32[]{:S(2)}) collective-permute-start(bf16[16,32,128]{2,1,0:T(8,128)(2,1)} %param.6), channel_id=1, source_target_pairs={{0,1},{1,0},{2,3},{3,2},{4,5},{5,4},{6,7},{7,6},{8,9},{9,8},{10,11... | collective-permute-start | bytes 393224 | tf_op jit(solution)/shard_map/ppermute | solution.py:62
  3.0 3.7 %collective-permute-done = bf16[16,32,128]{2,1,0:T(8,128)(2,1)S(1)} collective-permute-done((bf16[16,32,128]{2,1,0:T(8,128)(2,1)}, bf16[16,32,128]{2,1,0:T(8,128)(2,1)S(1)}, u32[]{:S(2)}, u32[]{:S(2)}) %collective-permute-start) | collective-permute-done | bytes 131104 | tf_op jit(solution)/shard_map/ppermute | solution.py:62
  6.7 1.0 maximum_select_fusion.4
  7.7 1.9 collective-permute-start.1
  9.6 5.6 %collective-permute-done.1 = bf16[32,32,128]{2,1,0:T(8,128)(2,1)S(1)} collective-permute-done((bf16[32,32,128]{2,1,0:T(8,128)(2,1)S(1)}, bf16[32,32,128]{2,1,0:T(8,128)(2,1)S(1)}, u32[]{:S(2)}, u32[]{:S(2)}) %collective-permute-start.1) | collective-permute-done | bytes 262176 | tf_op jit(solution)/shard_map/ppermute | solution.py:62
  15.3 2.6 collective-permute-start.2
  18.0 21.8 %collective-permute-done.2 = bf16[64,32,128]{2,1,0:T(8,128)(2,1)S(1)} collective-permute-done((bf16[64,32,128]{2,1,0:T(8,128)(2,1)S(1)}, bf16[64,32,128]{2,1,0:T(8,128)(2,1)S(1)}, u32[]{:S(2)}, u32[]{:S(2)}) %collective-permute-start.2) | collective-permute-done | bytes 524320 | tf_op jit(solution)/shard_map/ppermute | solution.py:62
  40.0 2.8 collective-permute-done.3
  42.8 2.0 maximum_select_fusion.1
  44.8 1.3 collective-permute-start.4
  46.2 13.6 %gather_fusion = s32[2560]{0:T(1024)S(1)} fusion(s32[2048]{0:T(1024)S(1)} %copy-done, s32[3072]{0:T(1024)S(1)} %pad_clamp_fusion), kind=kCustom, calls=%fused_computation | custom fusion | bytes 30720 | tf_op jit(solution)/shard_map/gather | solution.py:43
  60.7 1.0 scatter_custom_fusion
  61.8 0.7 copy.19
  62.5 4.8 %all-to-all-start.1 = ((s32[12,32,1]{0,2,1:T(1,128)}), s32[12,32,1]{0,2,1:T(1,128)S(1)}, u32[]{:S(2)}, u32[]{:S(2)}) async-start(s32[12,32,1]{0,2,1:T(1,128)} %copy.19), calls=%async_computation.1 | async-start | bytes 32768 | tf_op jit(solution)/shard_map/all_to_all | solution.py:71
  67.4 1.1 gather_fusion.1
  68.6 0.8 reshape.105
  69.4 23.4 %all-to-all-done.1 = s32[12,32,1]{0,2,1:T(1,128)S(1)} async-done(((s32[12,32,1]{0,2,1:T(1,128)}), s32[12,32,1]{0,2,1:T(1,128)S(1)}, u32[]{:S(2)}, u32[]{:S(2)}) %all-to-all-start.1) | async-done | bytes 1568 | tf_op jit(solution)/shard_map/all_to_all | solution.py:71
  92.8 5.4 %all-to-all-start = ((s32[32,1,240]{2,1,0:T(1,128)}), s32[32,1,240]{2,1,0:T(1,128)S(1)}, u32[]{:S(2)}, u32[]{:S(2)}) async-start(s32[32,1,240]{2,1,0:T(1,128)} %reshape.105), calls=%async_computation | async-start | bytes 65536 | tf_op jit(solution)/shard_map/all_to_all | solution.py:74
  98.4 7.0 %all-to-all-done = s32[32,1,240]{2,1,0:T(1,128)S(1)} async-done(((s32[32,1,240]{2,1,0:T(1,128)}), s32[32,1,240]{2,1,0:T(1,128)S(1)}, u32[]{:S(2)}, u32[]{:S(2)}) %all-to-all-start) | async-done | bytes 30752 | tf_op jit(solution)/shard_map/all_to_all | solution.py:74
  105.4 0.5 broadcast.119
  105.9 0.7 reduce.4
  106.9 4.1 %maximum_select_fusion = bf16[512,32,128]{2,1,0:T(8,128)(2,1)} fusion(bf16[256,32,128]{2,1,0:T(8,128)(2,1)} %collective-permute-done.4, bf16[256,32,128]{2,1,0:T(8,128)(2,1)S(1)} %maximum_select_fusion.1, pred[]{:T(512)S(6)} %eq.51), kind=kLoop, calls=%fused_computation.15 | loop fusion | flops 6291456 | bytes 8388609 | tf_op jit(solution)/shard_map/jit(_where)/select_n | solution.py:65
  111.0 5.0 %gather_fusion.2 = bf16[384,32,128]{2,1,0:T(8,128)(2,1)} fusion(bf16[512,32,128]{2,1,0:T(8,128)(2,1)} %maximum_select_fusion, s32[1024]{0:T(1024)S(1)} %pad_clamp_fusion.2), kind=kCustom, calls=%fused_computation.2 | custom fusion | bytes 6292992 | tf_op jit(solution)/shard_map/gather | solution.py:77
  116.0 148.1 %while.11 = (s32[]{:T(128)}, f32[24,16,20]{2,1,0:T(8,128)S(1)}, s32[24,16,20]{2,1,0:T(8,128)S(1)}, bf16[24,16,32,128]{3,2,1,0:T(8,128)(2,1)}, bf16[4096,128]{1,0:T(8,128)(2,1)S(1)}, /*index=5*/s32[]{:T(128)}, f32[]{:T(128)}) while((s32[]{:T(128)}, f32[24,16,20]{2,1,0:T(8,128)S(1)}, s32[24,16,20]{2,1,0:T(8,128)S(1)}, ...), condition=%wide.region_7.8_spmd.clone, body=%wide.region_3.7_spmd.clone.sunk | while | flops 539029184 | bytes 1485401 | solution.py:31
  116.0 5.5 %convolution_reduce_fusion.2 = f32[16,32,64]{1,2,0:T(8,128)S(1)} fusion(bf16[64,64,128,1]{2,1,0,3:T(8,128)(2,1)S(1)} %bitcast.52, bf16[24,16,32,128]{3,2,1,0:T(8,128)(2,1)} %get-tuple-element.110, s32[]{:T(128)} %get-tuple-element.100), kind=kOutput, calls=%fused_computation.6.clone.1 | convolution fusion | flops 538935296 | bytes 1311232 | tf_op jit(solution)/shard_map/while/body/eval_jaxpr/vqd,sd->vqs/dot_general | solution.py:21
  121.5 0.2 reduce_sum.35
  122.1 5.5 %convolution_reduce_fusion.2 = f32[16,32,64]{1,2,0:T(8,128)S(1)} fusion(bf16[64,64,128,1]{2,1,0,3:T(8,128)(2,1)S(1)} %bitcast.52, bf16[24,16,32,128]{3,2,1,0:T(8,128)(2,1)} %get-tuple-element.110, s32[]{:T(128)} %get-tuple-element.100), kind=kOutput, calls=%fused_computation.6.clone.1 | convolution fusion | flops 538935296 | bytes 1311232 | tf_op jit(solution)/shard_map/while/body/eval_jaxpr/vqd,sd->vqs/dot_general | solution.py:21
  127.7 0.2 reduce_sum.35
  128.3 5.5 %convolution_reduce_fusion.2 = f32[16,32,64]{1,2,0:T(8,128)S(1)} fusion(bf16[64,64,128,1]{2,1,0,3:T(8,128)(2,1)S(1)} %bitcast.52, bf16[24,16,32,128]{3,2,1,0:T(8,128)(2,1)} %get-tuple-element.110, s32[]{:T(128)} %get-tuple-element.100), kind=kOutput, calls=%fused_computation.6.clone.1 | convolution fusion | flops 538935296 | bytes 1311232 | tf_op jit(solution)/shard_map/while/body/eval_jaxpr/vqd,sd->vqs/dot_general | solution.py:21
  133.8 0.2 reduce_sum.35
  134.5 5.5 %convolution_reduce_fusion.2 = f32[16,32,64]{1,2,0:T(8,128)S(1)} fusion(bf16[64,64,128,1]{2,1,0,3:T(8,128)(2,1)S(1)} %bitcast.52, bf16[24,16,32,128]{3,2,1,0:T(8,128)(2,1)} %get-tuple-element.110, s32[]{:T(128)} %get-tuple-element.100), kind=kOutput, calls=%fused_computation.6.clone.1 | convolution fusion | flops 538935296 | bytes 1311232 | tf_op jit(solution)/shard_map/while/body/eval_jaxpr/vqd,sd->vqs/dot_general | solution.py:21
  140.0 0.2 reduce_sum.35
  140.6 5.5 %convolution_reduce_fusion.2 = f32[16,32,64]{1,2,0:T(8,128)S(1)} fusion(bf16[64,64,128,1]{2,1,0,3:T(8,128)(2,1)S(1)} %bitcast.52, bf16[24,16,32,128]{3,2,1,0:T(8,128)(2,1)} %get-tuple-element.110, s32[]{:T(128)} %get-tuple-element.100), kind=kOutput, calls=%fused_computation.6.clone.1 | convolution fusion | flops 538935296 | bytes 1311232 | tf_op jit(solution)/shard_map/while/body/eval_jaxpr/vqd,sd->vqs/dot_general | solution.py:21
  146.2 0.2 reduce_sum.35
  146.8 5.5 %convolution_reduce_fusion.2 = f32[16,32,64]{1,2,0:T(8,128)S(1)} fusion(bf16[64,64,128,1]{2,1,0,3:T(8,128)(2,1)S(1)} %bitcast.52, bf16[24,16,32,128]{3,2,1,0:T(8,128)(2,1)} %get-tuple-element.110, s32[]{:T(128)} %get-tuple-element.100), kind=kOutput, calls=%fused_computation.6.clone.1 | convolution fusion | flops 538935296 | bytes 1311232 | tf_op jit(solution)/shard_map/while/body/eval_jaxpr/vqd,sd->vqs/dot_general | solution.py:21
  152.4 0.2 reduce_sum.35
  153.0 5.5 %convolution_reduce_fusion.2 = f32[16,32,64]{1,2,0:T(8,128)S(1)} fusion(bf16[64,64,128,1]{2,1,0,3:T(8,128)(2,1)S(1)} %bitcast.52, bf16[24,16,32,128]{3,2,1,0:T(8,128)(2,1)} %get-tuple-element.110, s32[]{:T(128)} %get-tuple-element.100), kind=kOutput, calls=%fused_computation.6.clone.1 | convolution fusion | flops 538935296 | bytes 1311232 | tf_op jit(solution)/shard_map/while/body/eval_jaxpr/vqd,sd->vqs/dot_general | solution.py:21
  159.1 5.5 %convolution_reduce_fusion.2 = f32[16,32,64]{1,2,0:T(8,128)S(1)} fusion(bf16[64,64,128,1]{2,1,0,3:T(8,128)(2,1)S(1)} %bitcast.52, bf16[24,16,32,128]{3,2,1,0:T(8,128)(2,1)} %get-tuple-element.110, s32[]{:T(128)} %get-tuple-element.100), kind=kOutput, calls=%fused_computation.6.clone.1 | convolution fusion | flops 538935296 | bytes 1311232 | tf_op jit(solution)/shard_map/while/body/eval_jaxpr/vqd,sd->vqs/dot_general | solution.py:21
  164.7 0.2 reduce_sum.35
  165.3 5.5 %convolution_reduce_fusion.2 = f32[16,32,64]{1,2,0:T(8,128)S(1)} fusion(bf16[64,64,128,1]{2,1,0,3:T(8,128)(2,1)S(1)} %bitcast.52, bf16[24,16,32,128]{3,2,1,0:T(8,128)(2,1)} %get-tuple-element.110, s32[]{:T(128)} %get-tuple-element.100), kind=kOutput, calls=%fused_computation.6.clone.1 | convolution fusion | flops 538935296 | bytes 1311232 | tf_op jit(solution)/shard_map/while/body/eval_jaxpr/vqd,sd->vqs/dot_general | solution.py:21
  171.5 5.5 %convolution_reduce_fusion.2 = f32[16,32,64]{1,2,0:T(8,128)S(1)} fusion(bf16[64,64,128,1]{2,1,0,3:T(8,128)(2,1)S(1)} %bitcast.52, bf16[24,16,32,128]{3,2,1,0:T(8,128)(2,1)} %get-tuple-element.110, s32[]{:T(128)} %get-tuple-element.100), kind=kOutput, calls=%fused_computation.6.clone.1 | convolution fusion | flops 538935296 | bytes 1311232 | tf_op jit(solution)/shard_map/while/body/eval_jaxpr/vqd,sd->vqs/dot_general | solution.py:21
  177.0 0.2 reduce_sum.35
  177.7 5.5 %convolution_reduce_fusion.2 = f32[16,32,64]{1,2,0:T(8,128)S(1)} fusion(bf16[64,64,128,1]{2,1,0,3:T(8,128)(2,1)S(1)} %bitcast.52, bf16[24,16,32,128]{3,2,1,0:T(8,128)(2,1)} %get-tuple-element.110, s32[]{:T(128)} %get-tuple-element.100), kind=kOutput, calls=%fused_computation.6.clone.1 | convolution fusion | flops 538935296 | bytes 1311232 | tf_op jit(solution)/shard_map/while/body/eval_jaxpr/vqd,sd->vqs/dot_general | solution.py:21
  183.2 0.2 reduce_sum.35
  183.8 5.5 %convolution_reduce_fusion.2 = f32[16,32,64]{1,2,0:T(8,128)S(1)} fusion(bf16[64,64,128,1]{2,1,0,3:T(8,128)(2,1)S(1)} %bitcast.52, bf16[24,16,32,128]{3,2,1,0:T(8,128)(2,1)} %get-tuple-element.110, s32[]{:T(128)} %get-tuple-element.100), kind=kOutput, calls=%fused_computation.6.clone.1 | convolution fusion | flops 538935296 | bytes 1311232 | tf_op jit(solution)/shard_map/while/body/eval_jaxpr/vqd,sd->vqs/dot_general | solution.py:21
  190.0 5.5 %convolution_reduce_fusion.2 = f32[16,32,64]{1,2,0:T(8,128)S(1)} fusion(bf16[64,64,128,1]{2,1,0,3:T(8,128)(2,1)S(1)} %bitcast.52, bf16[24,16,32,128]{3,2,1,0:T(8,128)(2,1)} %get-tuple-element.110, s32[]{:T(128)} %get-tuple-element.100), kind=kOutput, calls=%fused_computation.6.clone.1 | convolution fusion | flops 538935296 | bytes 1311232 | tf_op jit(solution)/shard_map/while/body/eval_jaxpr/vqd,sd->vqs/dot_general | solution.py:21
  196.2 5.5 %convolution_reduce_fusion.2 = f32[16,32,64]{1,2,0:T(8,128)S(1)} fusion(bf16[64,64,128,1]{2,1,0,3:T(8,128)(2,1)S(1)} %bitcast.52, bf16[24,16,32,128]{3,2,1,0:T(8,128)(2,1)} %get-tuple-element.110, s32[]{:T(128)} %get-tuple-element.100), kind=kOutput, calls=%fused_computation.6.clone.1 | convolution fusion | flops 538935296 | bytes 1311232 | tf_op jit(solution)/shard_map/while/body/eval_jaxpr/vqd,sd->vqs/dot_general | solution.py:21
  202.4 5.5 %convolution_reduce_fusion.2 = f32[16,32,64]{1,2,0:T(8,128)S(1)} fusion(bf16[64,64,128,1]{2,1,0,3:T(8,128)(2,1)S(1)} %bitcast.52, bf16[24,16,32,128]{3,2,1,0:T(8,128)(2,1)} %get-tuple-element.110, s32[]{:T(128)} %get-tuple-element.100), kind=kOutput, calls=%fused_computation.6.clone.1 | convolution fusion | flops 538935296 | bytes 1311232 | tf_op jit(solution)/shard_map/while/body/eval_jaxpr/vqd,sd->vqs/dot_general | solution.py:21
  208.5 5.5 %convolution_reduce_fusion.2 = f32[16,32,64]{1,2,0:T(8,128)S(1)} fusion(bf16[64,64,128,1]{2,1,0,3:T(8,128)(2,1)S(1)} %bitcast.52, bf16[24,16,32,128]{3,2,1,0:T(8,128)(2,1)} %get-tuple-element.110, s32[]{:T(128)} %get-tuple-element.100), kind=kOutput, calls=%fused_computation.6.clone.1 | convolution fusion | flops 538935296 | bytes 1311232 | tf_op jit(solution)/shard_map/while/body/eval_jaxpr/vqd,sd->vqs/dot_general | solution.py:21
  214.7 5.5 %convolution_reduce_fusion.2 = f32[16,32,64]{1,2,0:T(8,128)S(1)} fusion(bf16[64,64,128,1]{2,1,0,3:T(8,128)(2,1)S(1)} %bitcast.52, bf16[24,16,32,128]{3,2,1,0:T(8,128)(2,1)} %get-tuple-element.110, s32[]{:T(128)} %get-tuple-element.100), kind=kOutput, calls=%fused_computation.6.clone.1 | convolution fusion | flops 538935296 | bytes 1311232 | tf_op jit(solution)/shard_map/while/body/eval_jaxpr/vqd,sd->vqs/dot_general | solution.py:21
  220.9 5.5 %convolution_reduce_fusion.2 = f32[16,32,64]{1,2,0:T(8,128)S(1)} fusion(bf16[64,64,128,1]{2,1,0,3:T(8,128)(2,1)S(1)} %bitcast.52, bf16[24,16,32,128]{3,2,1,0:T(8,128)(2,1)} %get-tuple-element.110, s32[]{:T(128)} %get-tuple-element.100), kind=kOutput, calls=%fused_computation.6.clone.1 | convolution fusion | flops 538935296 | bytes 1311232 | tf_op jit(solution)/shard_map/while/body/eval_jaxpr/vqd,sd->vqs/dot_general | solution.py:21
  227.0 5.5 %convolution_reduce_fusion.2 = f32[16,32,64]{1,2,0:T(8,128)S(1)} fusion(bf16[64,64,128,1]{2,1,0,3:T(8,128)(2,1)S(1)} %bitcast.52, bf16[24,16,32,128]{3,2,1,0:T(8,128)(2,1)} %get-tuple-element.110, s32[]{:T(128)} %get-tuple-element.100), kind=kOutput, calls=%fused_computation.6.clone.1 | convolution fusion | flops 538935296 | bytes 1311232 | tf_op jit(solution)/shard_map/while/body/eval_jaxpr/vqd,sd->vqs/dot_general | solution.py:21
  233.2 5.5 %convolution_reduce_fusion.2 = f32[16,32,64]{1,2,0:T(8,128)S(1)} fusion(bf16[64,64,128,1]{2,1,0,3:T(8,128)(2,1)S(1)} %bitcast.52, bf16[24,16,32,128]{3,2,1,0:T(8,128)(2,1)} %get-tuple-element.110, s32[]{:T(128)} %get-tuple-element.100), kind=kOutput, calls=%fused_computation.6.clone.1 | convolution fusion | flops 538935296 | bytes 1311232 | tf_op jit(solution)/shard_map/while/body/eval_jaxpr/vqd,sd->vqs/dot_general | solution.py:21
  239.4 5.5 %convolution_reduce_fusion.2 = f32[16,32,64]{1,2,0:T(8,128)S(1)} fusion(bf16[64,64,128,1]{2,1,0,3:T(8,128)(2,1)S(1)} %bitcast.52, bf16[24,16,32,128]{3,2,1,0:T(8,128)(2,1)} %get-tuple-element.110, s32[]{:T(128)} %get-tuple-element.100), kind=kOutput, calls=%fused_computation.6.clone.1 | convolution fusion | flops 538935296 | bytes 1311232 | tf_op jit(solution)/shard_map/while/body/eval_jaxpr/vqd,sd->vqs/dot_general | solution.py:21
  245.6 5.5 %convolution_reduce_fusion.2 = f32[16,32,64]{1,2,0:T(8,128)S(1)} fusion(bf16[64,64,128,1]{2,1,0,3:T(8,128)(2,1)S(1)} %bitcast.52, bf16[24,16,32,128]{3,2,1,0:T(8,128)(2,1)} %get-tuple-element.110, s32[]{:T(128)} %get-tuple-element.100), kind=kOutput, calls=%fused_computation.6.clone.1 | convolution fusion | flops 538935296 | bytes 1311232 | tf_op jit(solution)/shard_map/while/body/eval_jaxpr/vqd,sd->vqs/dot_general | solution.py:21
  251.7 5.5 %convolution_reduce_fusion.2 = f32[16,32,64]{1,2,0:T(8,128)S(1)} fusion(bf16[64,64,128,1]{2,1,0,3:T(8,128)(2,1)S(1)} %bitcast.52, bf16[24,16,32,128]{3,2,1,0:T(8,128)(2,1)} %get-tuple-element.110, s32[]{:T(128)} %get-tuple-element.100), kind=kOutput, calls=%fused_computation.6.clone.1 | convolution fusion | flops 538935296 | bytes 1311232 | tf_op jit(solution)/shard_map/while/body/eval_jaxpr/vqd,sd->vqs/dot_general | solution.py:21
  257.9 5.5 %convolution_reduce_fusion.2 = f32[16,32,64]{1,2,0:T(8,128)S(1)} fusion(bf16[64,64,128,1]{2,1,0,3:T(8,128)(2,1)S(1)} %bitcast.52, bf16[24,16,32,128]{3,2,1,0:T(8,128)(2,1)} %get-tuple-element.110, s32[]{:T(128)} %get-tuple-element.100), kind=kOutput, calls=%fused_computation.6.clone.1 | convolution fusion | flops 538935296 | bytes 1311232 | tf_op jit(solution)/shard_map/while/body/eval_jaxpr/vqd,sd->vqs/dot_general | solution.py:21
  264.2 0.8 reshape.107
  265.0 2.6 all-to-all-start.2
  267.6 7.2 %all-to-all-done.2 = f32[32,1,240]{2,1,0:T(1,128)S(1)} async-done(((f32[32,1,240]{2,1,0:T(1,128)}), f32[32,1,240]{2,1,0:T(1,128)S(1)}, u32[]{:S(2)}, u32[]{:S(2)}) %all-to-all-start.2) | async-done | bytes 30752 | tf_op jit(solution)/shard_map/all_to_all | solution.py:33
  274.7 0.5 broadcast.120
  275.3 0.7 reduce.5
  276.2 0.6 gather_fusion.3
  276.8 0.7 reshape.52
  (197 shorter events, 14.7 us)
Async XLA Ops:
  0.0 46.1 %copy-start = (s32[2048]{0:T(1024)S(1)}, s32[2048]{0:T(1024)}, u32[]{:S(2)}) copy-start(s32[2048]{0:T(1024)} %param.9) | copy-start | bytes 24580
  0.0 6.7 %collective-permute-start = (bf16[16,32,128]{2,1,0:T(8,128)(2,1)}, bf16[16,32,128]{2,1,0:T(8,128)(2,1)S(1)}, u32[]{:S(2)}, u32[]{:S(2)}) collective-permute-start(bf16[16,32,128]{2,1,0:T(8,128)(2,1)} %param.6), channel_id=1, source_target_pairs={{0,1},{1,0},{2,3},{3,2},{4,5},{5,4},{6,7},{7,6},{8,9},{9,8},{10,11... | collective-permute-start | bytes 393224 | tf_op jit(solution)/shard_map/ppermute | solution.py:62
  7.7 7.5 %collective-permute-start.1 = (bf16[32,32,128]{2,1,0:T(8,128)(2,1)S(1)}, bf16[32,32,128]{2,1,0:T(8,128)(2,1)S(1)}, u32[]{:S(2)}, u32[]{:S(2)}) collective-permute-start(bf16[32,32,128]{2,1,0:T(8,128)(2,1)S(1)} %maximum_select_fusion.4), channel_id=1, source_target_pairs={{0,2},{1,3},{2,0},{3,1},{4,6},{5,7},{6,4},{7,5},{8,10},{9,11},{10,... | collective-permute-start | bytes 786440 | tf_op jit(solution)/shard_map/ppermute | solution.py:62
  15.3 24.4 %collective-permute-start.2 = (bf16[64,32,128]{2,1,0:T(8,128)(2,1)S(1)}, bf16[64,32,128]{2,1,0:T(8,128)(2,1)S(1)}, u32[]{:S(2)}, u32[]{:S(2)}) collective-permute-start(bf16[64,32,128]{2,1,0:T(8,128)(2,1)S(1)} %maximum_select_fusion.3), channel_id=1, source_target_pairs={{0,4},{1,5},{2,6},{3,7},{4,0},{5,1},{6,2},{7,3},{8,12},{9,13},{10,... | collective-permute-start | bytes 1572872 | tf_op jit(solution)/shard_map/ppermute | solution.py:62
  18.0 28.1 %copy-start.1 = (s32[16,160]{1,0:T(8,128)S(1)}, s32[16,160]{1,0:T(8,128)}, u32[]{:S(2)}) copy-start(s32[16,160]{1,0:T(8,128)} %param.8) | copy-start | bytes 30724
  39.9 2.9 %collective-permute-start.3 = (bf16[128,32,128]{2,1,0:T(8,128)(2,1)S(1)}, bf16[128,32,128]{2,1,0:T(8,128)(2,1)}, u32[]{:S(2)}, u32[]{:S(2)}) collective-permute-start(bf16[128,32,128]{2,1,0:T(8,128)(2,1)S(1)} %maximum_select_fusion.2), channel_id=1, source_target_pairs={{0,8},{1,9},{2,10},{3,11},{4,12},{5,13},{6,14},{7,15},{8,0},{9,1},... | collective-permute-start | bytes 3145736 | tf_op jit(solution)/shard_map/ppermute | solution.py:62
  44.8 62.1 %collective-permute-start.4 = (bf16[256,32,128]{2,1,0:T(8,128)(2,1)S(1)}, bf16[256,32,128]{2,1,0:T(8,128)(2,1)}, u32[]{:S(2)}, u32[]{:S(2)}) collective-permute-start(bf16[256,32,128]{2,1,0:T(8,128)(2,1)S(1)} %maximum_select_fusion.1), channel_id=1, source_target_pairs={{0,16},{1,17},{2,18},{3,19},{4,20},{5,21},{6,22},{7,23},{8,24},{9,... | collective-permute-start | bytes 6291464 | tf_op jit(solution)/shard_map/ppermute | solution.py:62
  62.5 30.3 %all-to-all-start.1 = ((s32[12,32,1]{0,2,1:T(1,128)}), s32[12,32,1]{0,2,1:T(1,128)S(1)}, u32[]{:S(2)}, u32[]{:S(2)}) async-start(s32[12,32,1]{0,2,1:T(1,128)} %copy.19), calls=%async_computation.1 | async-start | bytes 32768 | tf_op jit(solution)/shard_map/all_to_all | solution.py:71
  92.8 12.6 %all-to-all-start = ((s32[32,1,240]{2,1,0:T(1,128)}), s32[32,1,240]{2,1,0:T(1,128)S(1)}, u32[]{:S(2)}, u32[]{:S(2)}) async-start(s32[32,1,240]{2,1,0:T(1,128)} %reshape.105), calls=%async_computation | async-start | bytes 65536 | tf_op jit(solution)/shard_map/all_to_all | solution.py:74
  111.0 5.0 %copy-start.2 = (bf16[64,64,128]{2,1,0:T(8,128)(2,1)S(1)}, bf16[64,64,128]{2,1,0:T(8,128)(2,1)}, u32[]{:S(2)}) copy-start(bf16[64,64,128]{2,1,0:T(8,128)(2,1)} %param.7) | copy-start | bytes 3145732
  265.0 9.8 %all-to-all-start.2 = ((f32[32,1,240]{2,1,0:T(1,128)}), f32[32,1,240]{2,1,0:T(1,128)S(1)}, u32[]{:S(2)}, u32[]{:S(2)}) async-start(f32[32,1,240]{2,1,0:T(1,128)} %reshape.107), calls=%async_computation.2 | async-start | bytes 65536 | tf_op jit(solution)/shard_map/all_to_all | solution.py:33
